TPU v7x, 32 devices: a whole 2x2x4 slice. The times are simulated.
32 devices in a mesh: tm: 8 (over y, x, core), chan: 4 (over z).
Axes of the slice: x: 2, y: 2, z: 4, core: 2. Of those that a mesh axis runs over, the one named last changes fastest.
Arguments:
- volts: bfloat16 [4, 16, 12288, 256], P(None, 'chan', 'tm'), may hold values from -6 to 6
- delay_peak: int32 [128, 128], P('tm', 'chan'), may hold values from 0 to 32767
- rate_peak: int32 [128, 128], P('tm', 'chan'), may hold values from 0 to 15
- station_order: int32 [128], replicated, may hold values from 0 to 127, each once
- ref_station: int32 [1], replicated, may hold values from 0 to 63
Outputs:
- fringe: float32 [128, 128, 2, 8], P('tm', 'chan')
- normal: float32 [128, 2, 256], P('tm', None, 'chan')
- rhs: float32 [128, 2], P('tm')
Inputs may be any that keep to these rules, and one draw needn't show every extreme that they name: `station_order`: each input appears once.
All inputs are finite; a program needn't handle non-finite values.
Results may differ from a plain program's by a relative error of at most 0.0003.
Values sent between devices are 32-bit elements; how exact they have to be, the bound alone decides.
A program may use at most 64 MiB of HBM per device.

v0:
```python
import math
import jax
import jax.numpy as jnp
from jax import lax
from jax.sharding import PartitionSpec as P

BAND = 16384
PERIODS_ALL = 8
WD = 4
WR = 2


def fringe_window(vis_re, vis_im, dpeak, rpeak, chans_total, periods):
    chan_local = vis_re.shape[3]
    dgrid = 2 * BAND
    rgrid = 2 * PERIODS_ALL
    dstep = BAND // chans_total
    rstep = PERIODS_ALL // periods
    chan_idx = jnp.arange(chan_local, dtype=jnp.int32)
    period_idx = jnp.arange(periods, dtype=jnp.int32)
    delays = dpeak[:, :, None] + (jnp.arange(WD, dtype=jnp.int32) - WD // 2) * dstep
    rates = rpeak[:, :, None] + (jnp.arange(WR, dtype=jnp.int32) - WR // 2) * rstep
    dphase = jnp.mod(delays[..., None] * chan_idx, dgrid).astype(jnp.float32) * (
        2.0 * math.pi / dgrid
    )
    rphase = jnp.mod(rates[..., None] * period_idx, rgrid).astype(jnp.float32) * (
        2.0 * math.pi / rgrid
    )
    angle = rphase[:, :, :, None, :, None] + dphase[:, :, None, :, None, :]
    cosine = jnp.cos(angle)
    sine = jnp.sin(angle)
    vr = vis_re[:, :, None, None]
    vi = vis_im[:, :, None, None]
    fre = jnp.sum(vr * cosine + vi * sine, axis=(4, 5))
    fim = jnp.sum(vi * cosine - vr * sine, axis=(4, 5))
    return (fre, fim)


def baseline_weights(fre, fim):
    power = fre * fre + fim * fim
    udel = (2.0 * jnp.arange(WD, dtype=jnp.float32) + 1.0 - WD) / WD
    urat = (2.0 * jnp.arange(WR, dtype=jnp.float32) + 1.0 - WR) / WR
    udel = udel[None, :]
    urat = urat[:, None]
    m_dd = jnp.mean(power * udel * udel, axis=(2, 3))
    m_dr = jnp.mean(power * udel * urat, axis=(2, 3))
    m_rr = jnp.mean(power * urat * urat, axis=(2, 3))
    g_d = jnp.mean(power * udel, axis=(2, 3))
    g_r = jnp.mean(power * urat, axis=(2, 3))
    return jnp.stack([m_dd, m_dr, m_rr, g_d, g_r])


def normal_terms(weights, row_inputs, col_inputs, inputs):
    slots = jnp.arange(inputs, dtype=jnp.int32)
    incidence = (row_inputs[:, None, None] == slots).astype(jnp.float32) - (
        col_inputs[None, :, None] == slots
    ).astype(jnp.float32)
    flat = incidence.reshape(-1, inputs)

    def block(weight):
        scaled = (incidence * weight[:, :, None]).reshape(-1, inputs)
        return jnp.dot(scaled.T, flat, precision=lax.Precision.HIGHEST) / inputs

    n_dd = block(weights[0])
    n_dr = block(weights[1])
    n_rr = block(weights[2])
    normal = jnp.concatenate(
        [jnp.concatenate([n_dd, n_dr], 1), jnp.concatenate([n_dr, n_rr], 1)], 0
    )
    rhs_d = jnp.dot(weights[3].reshape(-1), flat, precision=lax.Precision.HIGHEST) / inputs
    rhs_r = jnp.dot(weights[4].reshape(-1), flat, precision=lax.Precision.HIGHEST) / inputs
    return (normal, jnp.concatenate([rhs_d, rhs_r]))


def full_gram(volts, inputs, scale):
    prod = jnp.einsum("acti,actj->iacj", volts, volts, preferred_element_type=jnp.float32)
    real = prod[:inputs, :, :, :inputs] + prod[inputs:, :, :, inputs:]
    imag = prod[:inputs, :, :, inputs:] - prod[inputs:, :, :, :inputs]
    return jnp.stack([real, imag], axis=3) * scale


def body(volts, delay_peak, rate_peak, station_order, ref_station):
    periods, chans, samples, width = volts.shape
    inputs = width // 2
    row_count = delay_peak.shape[0]
    col_count = delay_peak.shape[1]
    time_devs = lax.axis_size("tm")
    chan_devs = lax.axis_size("chan")
    chans_total = chans * chan_devs
    scale = float(samples * time_devs) ** (-0.5)
    spread = float(periods * chans_total) ** (-0.5)
    col_inputs = lax.dynamic_slice_in_dim(
        station_order, lax.axis_index("chan") * col_count, col_count
    )
    row_inputs = lax.axis_index("tm") * row_count + jnp.arange(row_count, dtype=jnp.int32)
    gram = full_gram(volts, inputs, scale)
    summed = lax.psum_scatter(
        gram.reshape(lax.axis_size("tm") * row_count, -1), "tm", scatter_dimension=0, tiled=True
    )
    vis = summed.reshape(row_count, periods, chans, 2, inputs)
    grouped = jnp.take(vis, station_order, axis=4)
    moved = lax.all_to_all(grouped, "chan", split_axis=4, concat_axis=2, tiled=True)
    vis_re = jnp.transpose(moved[:, :, :, 0], (0, 3, 1, 2))
    vis_im = jnp.transpose(moved[:, :, :, 1], (0, 3, 1, 2))
    fre, fim = fringe_window(vis_re, vis_im, delay_peak, rate_peak, chans_total, periods)
    auto = (row_inputs[:, None] == col_inputs[None, :])[:, :, None, None]
    fre = jnp.where(auto, 0.0, fre * spread)
    fim = jnp.where(auto, 0.0, fim * spread)
    fringe = jnp.stack([fre, fim], axis=2).reshape(row_count, col_count, 2, WR * WD)
    weights = baseline_weights(fre, fim)
    col_width = 2 * inputs // chan_devs
    normal_part, rhs_part = normal_terms(weights, row_inputs, col_inputs, inputs)
    arranged = jnp.transpose(normal_part.reshape(2, inputs, 2 * inputs), (1, 0, 2))
    arranged = arranged.reshape(time_devs, row_count, 2, chan_devs, col_width)
    arranged = jnp.transpose(arranged, (0, 3, 1, 2, 4)).reshape(
        time_devs * chan_devs * row_count, 2, col_width
    )
    normal_rows = lax.psum_scatter(arranged, ("tm", "chan"), scatter_dimension=0, tiled=True)
    rhs_all = lax.psum(jnp.transpose(rhs_part.reshape(2, inputs), (1, 0)), ("tm", "chan"))
    rhs_rows = lax.dynamic_slice_in_dim(rhs_all, lax.axis_index("tm") * row_count, row_count, 0)
    columns = lax.axis_index("chan") * col_width + jnp.arange(col_width, dtype=jnp.int32)
    params = jnp.arange(2, dtype=jnp.int32)[None, :] * inputs + row_inputs[:, None]
    row_ref = row_inputs // 2 == ref_station[0]
    col_ref = columns % inputs // 2 == ref_station[0]
    ident = (params[:, :, None] == columns[None, None, :]).astype(jnp.float32)
    normal_rows = jnp.where(row_ref[:, None, None] | col_ref[None, None, :], ident, normal_rows)
    rhs_rows = jnp.where(row_ref[:, None], 0.0, rhs_rows)
    return (fringe, normal_rows, rhs_rows)


def solution(mesh):
    in_specs = (P(None, "chan", "tm", None), P("tm", "chan"), P("tm", "chan"), P(), P())
    out_specs = (P("tm", "chan", None, None), P("tm", None, "chan"), P("tm", None))
    return jax.shard_map(body, mesh=mesh, in_specs=in_specs, out_specs=out_specs, check_vma=False)
```

profile of v0, /device:TPU:0, one launch (start us, length us, event | category | flops | bytes accessed | tf_op | source)
XLA Modules:
  0.0 298.8 jit_solution(5013165204191400454)
XLA Ops:
  7.2 11.0 %convolution_bitcast_fusion = f32[256,4,4,256]{0,3,2,1:T(8,128)S(1)} fusion(bf16[4,4,1536,256]{3,2,1,0:T(8,128)(2,1)} %param.5), kind=kOutput, calls=%fused_computation.11 | convolution fusion | flops 3221225472 | bytes 16777216 | tf_op jit(solution)/shard_map/acti,actj->iacj/dot_general | solution.py:76
  19.0 1.9 copy.56
  22.3 42.6 %reduce-scatter.7.cloned.1.call-done = f32[16,4096]{1,0:T(8,128)} async-done(((f32[128,4096]{1,0:T(8,128)}), f32[16,4096]{1,0:T(8,128)}) %reduce-scatter.7.cloned.1.call-update) | async-done | bytes 262160
  64.9 1.5 copy.57
  66.5 2.7 copy.41
  69.2 4.9 %gather_fusion = f32[128,16,4,4,2]{1,3,4,2,0:T(4,128)} fusion(f32[16,4,4,2,128]{0,2,4,3,1:T(4,128)} %copy.41, s32[1024]{0:T(1024)S(1)} %pad_clamp_fusion), kind=kCustom, calls=%fused_computation | custom fusion | bytes 524800 | tf_op jit(solution)/shard_map/jit(_take)/gather | solution.py:101
  74.1 2.1 fusion.47
  76.2 2.3 reshape.374
  78.5 4.6 %all-to-all-start = ((f32[4,1,16384]{2,1,0:T(1,128)}), f32[4,1,16384]{2,1,0:T(1,128)S(1)}, u32[]{:S(2)}, u32[]{:S(2)}) async-start(f32[4,1,16384]{2,1,0:T(1,128)} %reshape.374), calls=%async_computation | async-start | bytes 524288 | tf_op jit(solution)/shard_map/all_to_all | solution.py:102
  83.1 1.0 fusion.22
  84.2 7.9 %all-to-all-done = f32[4,1,16384]{2,1,0:T(1,128)S(1)} async-done(((f32[4,1,16384]{2,1,0:T(1,128)}), f32[4,1,16384]{2,1,0:T(1,128)S(1)}, u32[]{:S(2)}, u32[]{:S(2)}) %all-to-all-start) | async-done | bytes 262176 | tf_op jit(solution)/shard_map/all_to_all | solution.py:102
  92.5 1.4 reduce
  93.9 1.5 reshape.375
  95.4 1.0 copy.42
  97.4 16.5 %fusion.5 = (f32[16,32,2,4]{1,3,2,0:T(4,128)S(1)}, f32[16,32,2,4]{1,3,2,0:T(4,128)S(1)}) fusion(f32[16,32,4,16]{1,3,2,0:T(8,128)S(1)} %copy.44, f32[16,32,4,16]{1,3,2,0:T(8,128)S(1)} %copy-done, f32[16,32,2,4]{1,3,2,0:T(4,128)S(1)} %fusion.41, f32[16,32,4,16]{1,3,2,0:T(8,128)S(1)} %copy.43), kind=kLoop, calls=%fused_computation.8 | loop fusion | flops 2351104 | bytes 442368 | tf_op jit(solution)/shard_map/reduce_sum | solution.py:34
  114.8 37.9 %psum.7 = f32[128,2]{0,1:T(2,128)S(1)} all-reduce(f32[128,2]{0,1:T(2,128)S(1)} %maximum_bitcast_fusion), channel_id=1, replica_groups=mesh['tm'=8,'chan'=4] {'tm','chan'}, use_global_device_ids=true, to_apply=%region_9.10 | all-reduce | flops 256 | bytes 2048 | tf_op jit(solution)/shard_map/psum | solution.py:119
  152.7 0.7 fusion.9
  153.4 0.7 fusion.8
  154.1 0.7 fusion.10
  155.2 0.8 copy.48
  156.0 0.7 pad_maximum_fusion
  156.7 0.6 dynamic-slice_select_fusion
  157.3 133.2 %reduce-scatter.5.cloned.1.call-done = f32[16,2,64]{2,0,1:T(8,128)} async-done(((f32[512,2,64]{2,0,1:T(8,128)}), f32[16,2,64]{2,0,1:T(8,128)}) %reduce-scatter.5.cloned.1.call-update) | async-done | bytes 8208 | tf_op jit(solution)/shard_map/reduce_scatter | solution.py:118
  290.6 0.8 convert_select_fusion
  (53 shorter events, 5.0 us)
Async XLA Ops:
  7.2 57.8 %reduce-scatter.7.cloned.1.call-start = ((), (), s32[]{:S(2)}) async-start(), calls=%async_computation.4 | async-start | bytes 2359296
  19.0 2.6 copy-start.3
  19.0 3.1 %copy-start.1 = (s32[16,32]{1,0:T(8,128)S(1)}, s32[16,32]{1,0:T(8,128)}, u32[]{:S(2)}) copy-start(s32[16,32]{1,0:T(8,128)} %param.7) | copy-start | bytes 6148
  19.0 3.2 %copy-start.2 = (s32[16,32]{1,0:T(8,128)S(1)}, s32[16,32]{1,0:T(8,128)}, u32[]{:S(2)}) copy-start(s32[16,32]{1,0:T(8,128)} %param.6) | copy-start | bytes 6148
  78.5 13.5 %all-to-all-start = ((f32[4,1,16384]{2,1,0:T(1,128)}), f32[4,1,16384]{2,1,0:T(1,128)S(1)}, u32[]{:S(2)}, u32[]{:S(2)}) async-start(f32[4,1,16384]{2,1,0:T(1,128)} %reshape.374), calls=%async_computation | async-start | bytes 524288 | tf_op jit(solution)/shard_map/all_to_all | solution.py:102
  83.1 207.5 %reduce-scatter.5.cloned.1.call-start = ((), (), s32[]{:S(2)}) async-start(), calls=%async_computation.3 | async-start | bytes 540672 | tf_op jit(solution)/shard_map/reduce_scatter | solution.py:118
  96.4 1.0 copy-start
Sparse Core Ops, SparseCore 0:
  21.0 43.8 reduce-scatter.6
  156.1 134.3 reduce-scatter.4
where the time goes:
time: 299 us
  waiting for transfers between devices  184 us (62%)
  blocking collectives  37.9 us (13%)
  other arithmetic  24.6 us (8%)
  local copies, waits for them, and re-layouts  19.4 us (6%)
  between operations  15 us (5%)
  matrix products  13.6 us (5%)
  starting transfers between devices  4.65 us (2%)
    reduce_scatter x1, waiting for transfers between devices, body(): lax.psum_scatter(arranged, ('tm', 'chan'), scatter_dimension=0, tiled=True)  133 us
    unnamed x3, waiting for transfers between devices  42.6 us
    psum x1, blocking collectives, body(): lax.psum(jnp.transpose(rhs_part.reshape(2, inputs), (1, 0)), ('tm', 'chan'))  37.9 us
    reduce_sum x1, other arithmetic, fringe_window(): fre = jnp.sum(vr * cosine + vi * sine, axis=(4, 5))  16.5 us
    dot_general x1, matrix products, full_gram(): jnp.einsum('acti,actj->iacj', volts, volts, preferred_element_type=jnp.fl...  11 us
    unnamed x13, local copies, waits for them, and re-layouts  8.36 us
    all_to_all x1, waiting for transfers between devices, body(): lax.all_to_all(grouped, 'chan', split_axis=4, concat_axis=2, tiled=True)  7.86 us
  transfers between devices with their start and end apart: 3, of which 3 were waited for; matrix products, arithmetic and copies ran while one was open for 1% of the time, Pallas kernels for 0%

commit v1 on v0

--- a/solution.py
+++ b/solution.py
@@ -8,6 +8,29 @@
 PERIODS_ALL = 8
 WD = 4
 WR = 2
+
+
+def cut_along(shard, dim, length):
+    lengths = shard.shape
+    tiles = shard.reshape(*lengths[:dim], length, lengths[dim] // length, *lengths[dim + 1 :])
+    return jnp.moveaxis(tiles, dim, 0)
+
+
+def in_order(blocks, dim):
+    dims = list(blocks.shape[1:])
+    dims[dim] *= blocks.shape[0]
+    return jnp.moveaxis(blocks, 0, dim).reshape(dims)
+
+
+def pairwise_exchange(value, axis, split_dim, concat_dim):
+    count, index = (lax.axis_size(axis), lax.axis_index(axis))
+    blocks = cut_along(value, split_dim, count)
+    outs = [blocks[index]]
+    for lap in range(1, count):
+        sent = blocks[index ^ lap]
+        outs.append(lax.ppermute(sent, axis, [(i, i ^ lap) for i in range(count)]))
+    blocks = jnp.stack(outs)[index ^ jnp.arange(count)]
+    return in_order(blocks, concat_dim)
 
 
 def fringe_window(vis_re, vis_im, dpeak, rpeak, chans_total, periods):
@@ -99,7 +122,7 @@
     )
     vis = summed.reshape(row_count, periods, chans, 2, inputs)
     grouped = jnp.take(vis, station_order, axis=4)
-    moved = lax.all_to_all(grouped, "chan", split_axis=4, concat_axis=2, tiled=True)
+    moved = pairwise_exchange(grouped, "chan", 4, 2)
     vis_re = jnp.transpose(moved[:, :, :, 0], (0, 3, 1, 2))
     vis_im = jnp.transpose(moved[:, :, :, 1], (0, 3, 1, 2))
     fre, fim = fringe_window(vis_re, vis_im, delay_peak, rate_peak, chans_total, periods)

time: 299 us -> 305 us (1.020)
  waiting for transfers between devices: 184 us -> 193 us
  blocking collectives: 37.9 us -> 43.1 us
  local copies, waits for them, and re-layouts: 19.4 us -> 14.9 us
  other arithmetic: 24.6 us -> 21 us
    ppermute x0 -> x3, waiting for transfers between devices: none -> 17.3 us  [pairwise_exchange(): outs.append(lax.ppermute(sent, axis, [(i, i ^ lap) for i in range(count)]))]
    all_to_all x1 -> x0, waiting for transfers between devices: 7.86 us -> none  [body(): lax.all_to_all(grouped, 'chan', split_axis=4, concat_axis=2, tiled=True)]
    psum x1, blocking collectives: 37.9 us -> 43.1 us  [body(): lax.psum(jnp.transpose(rhs_part.reshape(2, inputs), (1, 0)), ('tm', 'chan'))]
    all_to_all x1 -> x0, starting transfers between devices: 4.61 us -> none  [body(): lax.all_to_all(grouped, 'chan', split_axis=4, concat_axis=2, tiled=True)]
    unnamed x13 -> x9, local copies, waits for them, and re-layouts: 8.36 us -> 4.03 us
    ppermute x0 -> x3, starting transfers between devices: none -> 4.06 us  [pairwise_exchange(): outs.append(lax.ppermute(sent, axis, [(i, i ^ lap) for i in range(count)]))]
  transfers between devices with their start and end apart: 3 -> 5, of which waited for: 3 -> 4; matrix products, arithmetic and copies ran while one was open for 1% -> 1% of each run, Pallas kernels for 0% -> 0%
where the time goes in v1:
time: 305 us
  waiting for transfers between devices  193 us (63%)
  blocking collectives  43.1 us (14%)
  other arithmetic  21 us (7%)
  between operations  15.1 us (5%)
  local copies, waits for them, and re-layouts  14.9 us (5%)
  matrix products  13.6 us (4%)
  starting transfers between devices  4.33 us (1%)
    reduce_scatter x1, waiting for transfers between devices, body(): lax.psum_scatter(arranged, ('tm', 'chan'), scatter_dimension=0, tiled=True)  134 us
    psum x1, blocking collectives, body(): lax.psum(jnp.transpose(rhs_part.reshape(2, inputs), (1, 0)), ('tm', 'chan'))  43.1 us
    unnamed x3, waiting for transfers between devices  42 us
    ppermute x3, waiting for transfers between devices, pairwise_exchange(): outs.append(lax.ppermute(sent, axis, [(i, i ^ lap) for i in range(count)]))  17.3 us
    reduce_sum x1, other arithmetic, fringe_window(): fre = jnp.sum(vr * cosine + vi * sine, axis=(4, 5))  16.5 us
    dot_general x1, matrix products, full_gram(): jnp.einsum('acti,actj->iacj', volts, volts, preferred_element_type=jnp.fl...  11 us
  transfers between devices with their start and end apart: 5, of which 4 were waited for; matrix products, arithmetic and copies ran while one was open for 1% of the time, Pallas kernels for 0%

profile of v1, /device:TPU:0, one launch (start us, length us, event | category | flops | bytes accessed | tf_op | source)
XLA Modules:
  0.0 304.8 jit_solution(11636522455981821205)
XLA Ops:
  7.2 11.0 %convolution_bitcast_fusion = f32[256,4,4,256]{0,3,2,1:T(8,128)S(1)} fusion(bf16[4,4,1536,256]{3,2,1,0:T(8,128)(2,1)} %param.5), kind=kOutput, calls=%fused_computation.12 | convolution fusion | flops 3221225472 | bytes 16777216 | tf_op jit(solution)/shard_map/acti,actj->iacj/dot_general | solution.py:99
  19.0 1.9 copy.67
  23.0 41.9 %reduce-scatter.7.cloned.1.call-done = f32[16,4096]{1,0:T(8,128)} async-done(((f32[128,4096]{1,0:T(8,128)}), f32[16,4096]{1,0:T(8,128)}) %reduce-scatter.7.cloned.1.call-update) | async-done | bytes 262160
  64.9 1.5 copy.68
  66.5 2.7 copy.48
  69.2 3.8 %gather_fusion = f32[128,16,4,4,2]{1,3,4,2,0:T(4,128)S(1)} fusion(f32[16,4,4,2,128]{0,2,4,3,1:T(4,128)} %copy.48, s32[1024]{0:T(1024)S(1)} %pad_clamp_fusion.1), kind=kCustom, calls=%fused_computation | custom fusion | bytes 524800 | tf_op jit(solution)/shard_map/jit(_take)/gather | solution.py:124
  73.0 0.5 broadcast_select_fusion
  73.5 0.4 constant_dynamic-slice_fusion.4
  74.2 2.5 collective-permute-start.1
  77.0 1.5 collective-permute-start.2
  79.3 16.3 %collective-permute-done.1 = f32[16,4,4,2,32]{4,0,3,2,1:T(8,128)S(1)} collective-permute-done((f32[16,4,4,2,32]{4,0,3,2,1:T(8,128)S(1)}, f32[16,4,4,2,32]{4,0,3,2,1:T(8,128)S(1)}, u32[]{:S(2)}, u32[]{:S(2)}) %collective-permute-start.1) | collective-permute-done | bytes 65568 | tf_op jit(solution)/shard_map/ppermute | solution.py:31
  95.6 1.0 collective-permute-done
  96.7 0.6 gather_fusion.1
  97.9 16.5 %fusion.5 = (f32[16,32,2,4]{1,3,2,0:T(4,128)S(1)}, f32[16,32,2,4]{1,3,2,0:T(4,128)S(1)}) fusion(f32[16,32,4,16]{1,3,2,0:T(8,128)S(1)} %copy.55, f32[16,32,4,16]{1,3,2,0:T(8,128)S(1)} %fusion.22, f32[16,32,2,4]{1,3,2,0:T(4,128)S(1)} %fusion.41, f32[16,32,4,16]{1,3,2,0:T(8,128)S(1)} %copy.54), kind=kLoop, calls=%fused_computation.9 | loop fusion | flops 2351104 | bytes 442368 | tf_op jit(solution)/shard_map/reduce_sum | solution.py:57
  115.3 43.1 %psum.7 = f32[128,2]{0,1:T(2,128)S(1)} all-reduce(f32[128,2]{0,1:T(2,128)S(1)} %maximum_bitcast_fusion), channel_id=1, replica_groups=mesh['tm'=8,'chan'=4] {'tm','chan'}, use_global_device_ids=true, to_apply=%region_9.10 | all-reduce | flops 256 | bytes 2048 | tf_op jit(solution)/shard_map/psum | solution.py:142
  158.4 0.7 fusion.9
  159.1 0.7 fusion.8
  159.8 0.7 fusion.10
  160.9 0.8 copy.59
  161.7 0.7 pad_maximum_fusion.1
  162.4 0.6 fusion.44
  163.0 133.5 %reduce-scatter.5.cloned.1.call-done = f32[16,2,64]{2,0,1:T(8,128)} async-done(((f32[512,2,64]{2,0,1:T(8,128)}), f32[16,2,64]{2,0,1:T(8,128)}) %reduce-scatter.5.cloned.1.call-update) | async-done | bytes 8208 | tf_op jit(solution)/shard_map/reduce_scatter | solution.py:141
  296.6 0.8 convert_select_fusion
  297.4 0.6 copy.60
  (61 shorter events, 5.4 us)
Async XLA Ops:
  7.2 57.8 %reduce-scatter.7.cloned.1.call-start = ((), (), s32[]{:S(2)}) async-start(), calls=%async_computation.3 | async-start | bytes 2359296
  19.0 2.2 copy-start.2
  19.0 3.5 %copy-start = (s32[16,32]{1,0:T(8,128)S(1)}, s32[16,32]{1,0:T(8,128)}, u32[]{:S(2)}) copy-start(s32[16,32]{1,0:T(8,128)} %param.7) | copy-start | bytes 6148
  19.0 3.6 %copy-start.1 = (s32[16,32]{1,0:T(8,128)S(1)}, s32[16,32]{1,0:T(8,128)}, u32[]{:S(2)}) copy-start(s32[16,32]{1,0:T(8,128)} %param.6) | copy-start | bytes 6148
  20.9 275.7 %reduce-scatter.5.cloned.1.call-start = ((), (), s32[]{:S(2)}) async-start(), calls=%async_computation.2 | async-start | bytes 540672 | tf_op jit(solution)/shard_map/reduce_scatter | solution.py:141
  74.2 21.3 %collective-permute-start.1 = (f32[16,4,4,2,32]{4,0,3,2,1:T(8,128)S(1)}, f32[16,4,4,2,32]{4,0,3,2,1:T(8,128)S(1)}, u32[]{:S(2)}, u32[]{:S(2)}) collective-permute-start(f32[16,4,4,2,32]{4,0,3,2,1:T(8,128)S(1)} %bitcast.93), channel_id=1, source_target_pairs={{0,2},{1,3},{2,0},{3,1},{4,6},{5,7},{6,4},{7,5},{8,10},{9,11},{10,... | collective-permute-start | bytes 196616 | tf_op jit(solution)/shard_map/ppermute | solution.py:31
  77.0 18.5 %collective-permute-start.2 = (f32[16,4,4,2,32]{4,0,3,2,1:T(8,128)S(1)}, f32[16,4,4,2,32]{4,0,3,2,1:T(8,128)S(1)}, u32[]{:S(2)}, u32[]{:S(2)}) collective-permute-start(f32[16,4,4,2,32]{4,0,3,2,1:T(8,128)S(1)} %bitcast.94), channel_id=1, source_target_pairs={{0,3},{1,2},{2,1},{3,0},{4,7},{5,6},{6,5},{7,4},{8,11},{9,10},{10,... | collective-permute-start | bytes 196616 | tf_op jit(solution)/shard_map/ppermute | solution.py:31
  78.8 17.7 %collective-permute-start = (f32[16,4,4,2,32]{4,0,3,2,1:T(8,128)S(1)}, f32[16,4,4,2,32]{4,0,3,2,1:T(8,128)S(1)}, u32[]{:S(2)}, u32[]{:S(2)}) collective-permute-start(f32[16,4,4,2,32]{4,0,3,2,1:T(8,128)S(1)} %bitcast.95), channel_id=1, source_target_pairs={{0,1},{1,0},{2,3},{3,2},{4,5},{5,4},{6,7},{7,6},{8,9},{9,8},{10,11... | collective-permute-start | bytes 196616 | tf_op jit(solution)/shard_map/ppermute | solution.py:31
Sparse Core Ops, SparseCore 0:
  21.0 43.8 reduce-scatter.6
  161.8 134.6 reduce-scatter.4
